TPU v7x, 256 devices: a whole 4x4x8 slice. The times are simulated.
256 devices in a mesh: pts: 32 (over x, y, z_lo), grid: 8 (over z_hi, core).
Axes of the slice: x: 4, y: 4, z: 8 (z_hi: 4, z_lo: 2; z = z_hi * 2 + z_lo), core: 2. Of those that a mesh axis runs over, the one named last changes fastest.
Arguments:
- probes: bfloat16 [8, 1024, 8, 128], P('grid', 'pts'), may hold values from -6 to 6
- weights: bfloat16 [8, 1024, 64, 128], P('grid', 'pts'), may hold values from -0.049804688 to 0.25
- brick_owner: int32 [8, 1024, 1], P('grid', 'pts'), may hold values from 0 to 31; in each aligned block of 32 rows (0 to 31, 32 to 63, ..., all dimensions but the last counted through in order) at most 2 rows name the same one
- brick_slot: int32 [8, 1024], P('grid', 'pts'), may hold values from 0 to 127
- counts: int32 [8, 1024], P('grid', 'pts'), may hold values from 64 to 128
- length_scale: float32 [1], replicated, may hold values from 0.015 to 0.05
Outputs:
- covariance_product: float32 [8, 1024, 8, 128], P('grid', 'pts')
- lengthscale_adjoint: float32 [8, 1024, 8, 128], P('grid', 'pts')
Inputs may be any that keep to these rules, and one draw needn't show every extreme that they name: `brick_owner`: among the 32 blocks of one device, at most 2 have one owner, and some owner has exactly 2 of them.
All inputs are finite; a program needn't handle non-finite values.
Results may differ from a plain program's by a relative error of at most 0.0028.
Values may be sent and summed in bfloat16 or wider, within the bound.
A program may use at most 64 MiB of HBM per device.

v0:
```python
import math

import jax
import jax.numpy as jnp
from jax import lax
from jax.sharding import PartitionSpec as P

GX = 128
GY = 128
GZ = 128


ROOT_FIVE = math.sqrt(5.0)


def shortened(x):
    return jax.tree.map(lambda a: a.astype(jnp.bfloat16) if a.dtype == jnp.float32 else a, x)


def matern_tables(length_scale, extent):
    ell = length_scale[0]
    places = lax.broadcasted_iota(jnp.int32, (extent,), 0).astype(jnp.float32)
    spread = jnp.abs(places[:, None] - places[None, :]) / extent
    scaled = ROOT_FIVE * spread / ell
    decay = jnp.exp(-scaled)
    factor = 1.0 / jnp.sqrt(extent * ell)
    poly = 1.0 + scaled + scaled * scaled / 3.0
    value = poly * decay * factor
    slope = (scaled * scaled * (1.0 + scaled) / 3.0 - 0.5 * poly) * decay * factor
    return (value, slope)


def on_device(probes, weights, brick_owner, brick_slot, counts, length_scale):
    precise = lax.Precision.HIGHEST
    point_devs = lax.axis_size("pts")
    grid_devs = lax.axis_size("grid")
    blocks = probes.shape[1]
    probe_count = probes.shape[2]
    block_points = probes.shape[3]
    slab_x = GX // grid_devs
    brick_total = slab_x // 4 * (GY // 4) * (GZ // 4)
    own_bricks = brick_total // point_devs
    column_count = own_bricks // (GZ // 4)
    z_piece = GZ // point_devs
    capacity = max(2, (2 * blocks + point_devs - 1) // point_devs)
    row_width = probe_count * 64
    usable = (
        lax.broadcasted_iota(jnp.int32, (blocks, block_points), 1) < counts[0][:, None]
    ).astype(jnp.float32)
    masked = probes[0] * usable[:, None, :].astype(probes.dtype)
    partial_value = jnp.einsum(
        "bcn,bpn->bpc", weights[0], masked, preferred_element_type=jnp.float32
    ).reshape(blocks, row_width)
    owners = brick_owner[0][:, 0]
    choose = (owners[:, None] == lax.broadcasted_iota(jnp.int32, (blocks, point_devs), 1)).astype(
        jnp.int32
    )
    ranking = jnp.sum((jnp.cumsum(choose, axis=0) - 1) * choose, axis=1)
    target = owners * capacity + ranking
    outgoing = (
        jnp.zeros((point_devs * capacity, row_width), jnp.float32).at[target].set(partial_value)
    )
    labels = jnp.full((point_devs * capacity,), own_bricks, jnp.int32).at[target].set(brick_slot[0])
    arrived, arrived_labels = (
        lax.all_to_all(
            outgoing.astype(jnp.bfloat16), "pts", split_axis=0, concat_axis=0, tiled=True
        ).astype(outgoing.dtype),
        lax.all_to_all(labels, "pts", split_axis=0, concat_axis=0, tiled=True),
    )
    summed = jax.ops.segment_sum(arrived, arrived_labels, num_segments=own_bricks + 1)[:own_bricks]
    kx_value, kx_slope = matern_tables(length_scale, GX)
    ky_value, ky_slope = matern_tables(length_scale, GY)
    kz_value, kz_slope = matern_tables(length_scale, GZ)
    cubes = summed.reshape(column_count, GZ // 4, probe_count, 4, 4, 4)
    z_lines = cubes.transpose(0, 3, 4, 2, 1, 5).reshape(column_count * 16 * probe_count, GZ)
    along_z = jnp.dot(z_lines, kz_value, precision=precise)
    slope_z = jnp.dot(z_lines, kz_slope, precision=precise)

    def to_pieces(grid_part):
        shaped = grid_part.reshape(column_count, 4, 4, probe_count, point_devs, z_piece)
        return shaped.transpose(4, 0, 1, 2, 3, 5).reshape(
            point_devs, column_count * 16 * probe_count * z_piece
        )

    def to_rows(grid_part):
        shaped = grid_part.reshape(slab_x // 4, GY // 4, 4, 4, probe_count, z_piece)
        return shaped.transpose(0, 2, 4, 5, 1, 3).reshape(slab_x * probe_count * z_piece, GY)

    got_value, got_slope = (
        lax.all_to_all(
            to_pieces(along_z).astype(jnp.bfloat16), "pts", split_axis=0, concat_axis=0, tiled=True
        ).astype(jnp.float32),
        lax.all_to_all(
            to_pieces(slope_z).astype(jnp.bfloat16), "pts", split_axis=0, concat_axis=0, tiled=True
        ).astype(jnp.float32),
    )
    rows_value = to_rows(got_value)
    rows_slope = to_rows(got_slope)
    both_y = jnp.dot(rows_value, ky_value, precision=precise)
    mixed_y = jnp.dot(rows_value, ky_slope, precision=precise) + jnp.dot(
        rows_slope, ky_value, precision=precise
    )
    smooth_part = both_y.reshape(slab_x, probe_count, z_piece, GY)
    mixed_part = mixed_y.reshape(slab_x, probe_count, z_piece, GY)
    full_value, full_mixed = (
        lax.all_to_all(
            shortened(smooth_part), "grid", split_axis=1, concat_axis=0, tiled=True
        ).astype(smooth_part.dtype),
        lax.all_to_all(
            shortened(mixed_part), "grid", split_axis=1, concat_axis=0, tiled=True
        ).astype(mixed_part.dtype),
    )
    flat_value = full_value.reshape(GX, -1)
    flat_mixed = full_mixed.reshape(GX, -1)
    value_out = jnp.dot(kx_value, flat_value, precision=precise)
    slope_out = jnp.dot(kx_slope, flat_value, precision=precise) + jnp.dot(
        kx_value, flat_mixed, precision=precise
    )
    value_out = value_out.astype(jnp.bfloat16).reshape(GX, probe_count // grid_devs, z_piece, GY)
    slope_out = slope_out.astype(jnp.bfloat16).reshape(GX, probe_count // grid_devs, z_piece, GY)
    value_home, slope_home = (
        lax.all_to_all(value_out, "grid", split_axis=0, concat_axis=1, tiled=True),
        lax.all_to_all(slope_out, "grid", split_axis=0, concat_axis=1, tiled=True),
    )

    def from_rows(grid_part):
        shaped = grid_part.reshape(slab_x // 4, 4, probe_count, z_piece, GY // 4, 4)
        return shaped.transpose(0, 4, 1, 5, 2, 3).reshape(
            point_devs, column_count * 16 * probe_count * z_piece
        )

    def to_bricks(grid_part):
        shaped = grid_part.reshape(point_devs, column_count, 4, 4, probe_count, z_piece)
        lined = shaped.transpose(1, 2, 3, 4, 0, 5)
        return lined.transpose(0, 4, 3, 1, 2, 5).reshape(own_bricks, row_width)

    back_value, back_slope = (
        lax.all_to_all(from_rows(value_home), "pts", split_axis=0, concat_axis=0, tiled=True),
        lax.all_to_all(from_rows(slope_home), "pts", split_axis=0, concat_axis=0, tiled=True),
    )
    value_bricks = to_bricks(back_value)
    slope_bricks = to_bricks(back_slope)
    pick_rows = jnp.minimum(arrived_labels, own_bricks - 1)
    send_value = jnp.take(value_bricks, pick_rows, axis=0)
    send_slope = jnp.take(slope_bricks, pick_rows, axis=0)
    home_value, home_slope = (
        lax.all_to_all(send_value, "pts", split_axis=0, concat_axis=0, tiled=True),
        lax.all_to_all(send_slope, "pts", split_axis=0, concat_axis=0, tiled=True),
    )
    block_value = jnp.take(home_value, target, axis=0).reshape(blocks, probe_count, 64)
    block_slope = jnp.take(home_slope, target, axis=0).reshape(blocks, probe_count, 64)
    covariance_product = (
        jnp.einsum("bcn,bpc->bpn", weights[0], block_value, preferred_element_type=jnp.float32)
        * usable[:, None, :]
    )
    lengthscale_adjoint = (
        jnp.einsum("bcn,bpc->bpn", weights[0], block_slope, preferred_element_type=jnp.float32)
        * usable[:, None, :]
    )
    return (covariance_product[None], lengthscale_adjoint[None])


def solution(mesh):
    placed = (
        P("grid", "pts", None, None),
        P("grid", "pts", None, None),
        P("grid", "pts", None),
        P("grid", "pts"),
        P("grid", "pts"),
        P(),
    )
    return jax.shard_map(
        on_device,
        mesh=mesh,
        in_specs=placed,
        out_specs=(P("grid", "pts", None, None), P("grid", "pts", None, None)),
        check_vma=False,
    )
```

profile of v0, /device:TPU:64, one launch (start us, length us, event | category | flops | bytes accessed | tf_op | source)
XLA Modules:
  0.0 362.2 jit_solution(17619089322066202451)
XLA Ops:
  0.6 0.8 fusion.53
  1.5 0.8 select_reduce_fusion
  3.0 0.8 scatter_custom_fusion
  3.8 0.7 all_to_all.92
  4.5 8.7 %all-to-all-start = ((s32[32,2,1]{1,2,0:T(1,128)}), s32[32,2,1]{1,2,0:T(1,128)S(1)}, u32[]{:S(2)}, u32[]{:S(2)}) async-start(s32[32,2,1]{1,2,0:T(1,128)} %bitcast.5), calls=%async_computation | async-start | bytes 32768 | tf_op jit(solution)/shard_map/all_to_all | solution.py:68
  13.2 0.7 fusion.54
  13.9 1.2 fusion.8
  15.2 0.7 scatter_custom_fusion.1
  16.7 4.7 %all-to-all-done = s32[32,2,1]{1,2,0:T(1,128)S(1)} async-done(((s32[32,2,1]{1,2,0:T(1,128)}), s32[32,2,1]{1,2,0:T(1,128)S(1)}, u32[]{:S(2)}, u32[]{:S(2)}) %all-to-all-start) | async-done | bytes 288 | tf_op jit(solution)/shard_map/all_to_all | solution.py:68
  21.4 3.9 %all-to-all-start.1 = ((bf16[32,2,512]{2,1,0:T(2,128)(2,1)}), bf16[32,2,512]{2,1,0:T(2,128)(2,1)S(1)}, u32[]{:S(2)}, u32[]{:S(2)}) async-start(bf16[32,2,512]{2,1,0:T(2,128)(2,1)} %all_to_all.94), calls=%async_computation.1 | async-start | bytes 131072 | tf_op jit(solution)/shard_map/all_to_all | solution.py:65
  26.4 0.7 minimum_reduce_fusion
  27.3 6.3 %all-to-all-done.1 = bf16[32,2,512]{2,1,0:T(2,128)(2,1)S(1)} async-done(((bf16[32,2,512]{2,1,0:T(2,128)(2,1)}), bf16[32,2,512]{2,1,0:T(2,128)(2,1)S(1)}, u32[]{:S(2)}, u32[]{:S(2)}) %all-to-all-start.1) | async-done | bytes 65568 | tf_op jit(solution)/shard_map/all_to_all | solution.py:65
  33.6 1.0 scatter_custom_fusion.2
  35.2 3.2 copy.57
  38.4 14.9 %fusion = bf16[32,4,4,4,8,4]{0,4,5,3,2,1:T(8,128)(2,1)S(1)} fusion(f32[4,4,4,8,128,1]{3,4,5,2,1,0:T(8,128)} %bitcast.134, f32[]{:T(128)S(6)} %sqrt.2, f32[]{:T(128)} %bitcast.126, f32[32,4]{0,1:T(4,128)S(1)} %add_convert_fusion, f32[128]{0:T(128)S(1)} %iota_convert_fusion), kind=kOutput, calls=%fused_computation.9 | convolution fusion | flops 100909056 | bytes 394248 | tf_op jit(solution)/shard_map/dot_general | solution.py:76
  54.1 1.1 reduce.11
  55.4 0.7 reshape.366
  56.1 4.4 %all-to-all-start.2 = ((bf16[32,2,1024]{2,1,0:T(2,128)(2,1)}), bf16[32,2,1024]{2,1,0:T(2,128)(2,1)S(1)}, u32[]{:S(2)}, u32[]{:S(2)}) async-start(bf16[32,2,1024]{2,1,0:T(2,128)(2,1)} %reshape.366), calls=%async_computation.2 | async-start | bytes 262144 | tf_op jit(solution)/shard_map/all_to_all | solution.py:90
  60.5 14.9 %fusion.1 = bf16[32,4,4,4,8,4]{0,4,5,3,2,1:T(8,128)(2,1)S(1)} fusion(f32[4,4,4,8,128,1]{3,4,5,2,1,0:T(8,128)} %bitcast.135, f32[]{:T(128)S(6)} %sqrt.2, f32[]{:T(128)} %bitcast.125, f32[32,4]{0,1:T(4,128)S(1)} %add_convert_fusion, f32[128]{0:T(128)S(1)} %iota_convert_fusion), kind=kOutput, calls=%fused_computation.10 | convolution fusion | flops 100974592 | bytes 394248 | tf_op jit(solution)/shard_map/dot_general | solution.py:77
  75.7 1.1 reduce.12
  77.0 0.7 reshape.370
  77.7 8.6 %all-to-all-start.7 = ((bf16[32,2,1024]{2,1,0:T(2,128)(2,1)}), bf16[32,2,1024]{2,1,0:T(2,128)(2,1)S(1)}, u32[]{:S(2)}, u32[]{:S(2)}) async-start(bf16[32,2,1024]{2,1,0:T(2,128)(2,1)} %reshape.370), calls=%async_computation.7 | async-start | bytes 262144 | tf_op jit(solution)/shard_map/all_to_all | solution.py:93
  86.4 0.7 reduce.2
  87.1 10.0 %reshape.253 = bf16[4,32,4,4,8,4]{5,4,3,2,1,0:T(8,128)(2,1)} reshape(bf16[32,2048]{1,0:T(8,128)(2,1)S(1)} %reduce.2) | data formatting | bytes 262144 | tf_op jit(solution)/shard_map/reshape | solution.py:86
  97.2 15.4 %copy.61 = bf16[4,4,8,4,32,4]{2,5,4,3,1,0:T(4,128)(2,1)S(1)} copy(bf16[4,4,8,4,32,4]{3,2,5,1,4,0:T(8,128)(2,1)} %bitcast.136) | data formatting | bytes 262144 | tf_op jit(solution)/shard_map/transpose | solution.py:87
  112.5 31.7 %copy.72 = bf16[4,4,8,4,32,4]{5,4,3,2,1,0:T(8,128)(2,1)} copy(bf16[4,4,8,4,32,4]{3,2,5,1,4,0:T(8,128)(2,1)} %bitcast.137) | data formatting | bytes 262144 | tf_op jit(solution)/shard_map/transpose | solution.py:87
  144.3 0.7 reduce.3
  145.1 10.0 %reshape.261 = bf16[4,32,4,4,8,4]{5,4,3,2,1,0:T(8,128)(2,1)} reshape(bf16[32,2048]{1,0:T(8,128)(2,1)S(1)} %reduce.3) | data formatting | bytes 262144 | tf_op jit(solution)/shard_map/reshape | solution.py:86
  155.1 31.7 %copy.76 = bf16[4,4,8,4,32,4]{5,4,3,2,1,0:T(8,128)(2,1)} copy(bf16[4,4,8,4,32,4]{3,2,5,1,4,0:T(8,128)(2,1)} %bitcast.138) | data formatting | bytes 262144 | tf_op jit(solution)/shard_map/transpose | solution.py:87
  186.8 8.7 %reshape.262 = bf16[512,128]{1,0:T(8,128)(2,1)S(1)} reshape(bf16[4,4,8,4,32,4]{5,4,3,2,1,0:T(8,128)(2,1)} %copy.76) | data formatting | bytes 262144 | tf_op jit(solution)/shard_map/reshape | solution.py:87
  195.4 8.9 %reshape.260 = bf16[512,128]{1,0:T(8,128)(2,1)S(1)} reshape(bf16[4,4,8,4,32,4]{5,4,3,2,1,0:T(8,128)(2,1)} %copy.72) | data formatting | bytes 262144 | tf_op jit(solution)/shard_map/reshape | solution.py:87
  204.4 1.8 convolution_convert_fusion.3
  206.2 0.7 copy.63
  206.9 7.2 %all-to-all-start.3 = ((bf16[16,8,4,128]{3,2,0,1:T(4,128)(2,1)}), bf16[16,8,4,128]{3,2,0,1:T(4,128)(2,1)S(1)}, u32[]{:S(2)}, u32[]{:S(2)}) async-start(bf16[16,8,4,128]{3,2,0,1:T(4,128)(2,1)} %copy.63), calls=%async_computation.3 | async-start | bytes 262144 | tf_op jit(solution)/shard_map/all_to_all | solution.py:106
  214.8 0.7 copy.77
  215.5 4.8 %all-to-all-done.3 = bf16[16,8,4,128]{3,2,0,1:T(4,128)(2,1)S(1)} async-done(((bf16[16,8,4,128]{3,2,0,1:T(4,128)(2,1)}), bf16[16,8,4,128]{3,2,0,1:T(4,128)(2,1)S(1)}, u32[]{:S(2)}, u32[]{:S(2)}) %all-to-all-start.3) | async-done | bytes 131104 | tf_op jit(solution)/shard_map/all_to_all | solution.py:106
  220.4 6.9 %all-to-all-start.8 = ((bf16[16,8,4,128]{3,2,0,1:T(4,128)(2,1)}), bf16[16,8,4,128]{3,2,0,1:T(4,128)(2,1)S(1)}, u32[]{:S(2)}, u32[]{:S(2)}) async-start(bf16[16,8,4,128]{3,2,0,1:T(4,128)(2,1)} %copy.77), calls=%async_computation.8 | async-start | bytes 262144 | tf_op jit(solution)/shard_map/all_to_all | solution.py:109
  228.7 6.4 %all-to-all-done.8 = bf16[16,8,4,128]{3,2,0,1:T(4,128)(2,1)S(1)} async-done(((bf16[16,8,4,128]{3,2,0,1:T(4,128)(2,1)}), bf16[16,8,4,128]{3,2,0,1:T(4,128)(2,1)S(1)}, u32[]{:S(2)}, u32[]{:S(2)}) %all-to-all-start.8) | async-done | bytes 131104 | tf_op jit(solution)/shard_map/all_to_all | solution.py:109
  235.1 5.3 %all-to-all-start.4 = ((bf16[128,1,4,128]{3,2,1,0:T(4,128)(2,1)}), bf16[128,1,4,128]{3,2,1,0:T(4,128)(2,1)S(1)}, u32[]{:S(2)}, u32[]{:S(2)}) async-start(bf16[128,1,4,128]{3,2,1,0:T(4,128)(2,1)} %bitcast.23), calls=%async_computation.4 | async-start | bytes 262144 | tf_op jit(solution)/shard_map/all_to_all | solution.py:122
  240.7 0.7 reshape.264
  241.4 6.5 %all-to-all-done.4 = bf16[128,1,4,128]{3,2,1,0:T(4,128)(2,1)S(1)} async-done(((bf16[128,1,4,128]{3,2,1,0:T(4,128)(2,1)}), bf16[128,1,4,128]{3,2,1,0:T(4,128)(2,1)S(1)}, u32[]{:S(2)}, u32[]{:S(2)}) %all-to-all-start.4) | async-done | bytes 131104 | tf_op jit(solution)/shard_map/all_to_all | solution.py:122
  248.0 5.3 %all-to-all-start.9 = ((bf16[128,1,4,128]{3,2,1,0:T(4,128)(2,1)}), bf16[128,1,4,128]{3,2,1,0:T(4,128)(2,1)S(1)}, u32[]{:S(2)}, u32[]{:S(2)}) async-start(bf16[128,1,4,128]{3,2,1,0:T(4,128)(2,1)} %bitcast.40), calls=%async_computation.9 | async-start | bytes 262144 | tf_op jit(solution)/shard_map/all_to_all | solution.py:123
  253.3 1.1 copy.66
  254.4 14.5 %copy.67 = bf16[4,32,4,4,8,4]{5,4,3,2,1,0:T(8,128)(2,1)} copy(bf16[4,32,4,4,8,4]{4,3,1,5,2,0:T(4,128)(2,1)S(1)} %bitcast.140) | data formatting | bytes 262144 | tf_op jit(solution)/shard_map/transpose | solution.py:128
  268.9 8.5 %all_to_all.120 = bf16[32,1,2048]{2,1,0:T(2,128)(2,1)S(1)} reshape(bf16[4,32,4,4,8,4]{5,4,3,2,1,0:T(8,128)(2,1)} %copy.67) | data formatting | bytes 262144 | tf_op jit(solution)/shard_map/all_to_all | solution.py:138
  277.3 1.3 reduce.14
  278.7 0.7 reshape.368
  279.4 8.0 %all-to-all-start.5 = ((bf16[32,2,1024]{2,1,0:T(2,128)(2,1)}), bf16[32,2,1024]{2,1,0:T(2,128)(2,1)S(1)}, u32[]{:S(2)}, u32[]{:S(2)}) async-start(bf16[32,2,1024]{2,1,0:T(2,128)(2,1)} %reshape.368), calls=%async_computation.5 | async-start | bytes 262144 | tf_op jit(solution)/shard_map/all_to_all | solution.py:138
  287.6 1.1 copy.80
  288.7 14.5 %copy.81 = bf16[4,32,4,4,8,4]{5,4,3,2,1,0:T(8,128)(2,1)} copy(bf16[4,32,4,4,8,4]{4,3,1,5,2,0:T(4,128)(2,1)S(1)} %bitcast.141) | data formatting | bytes 262144 | tf_op jit(solution)/shard_map/transpose | solution.py:128
  303.1 8.5 %all_to_all.121 = bf16[32,1,2048]{2,1,0:T(2,128)(2,1)S(1)} reshape(bf16[4,32,4,4,8,4]{5,4,3,2,1,0:T(8,128)(2,1)} %copy.81) | data formatting | bytes 262144 | tf_op jit(solution)/shard_map/all_to_all | solution.py:139
  311.6 1.3 reduce.13
  313.0 0.7 reshape.372
  313.7 8.4 %all-to-all-start.10 = ((bf16[32,2,1024]{2,1,0:T(2,128)(2,1)}), bf16[32,2,1024]{2,1,0:T(2,128)(2,1)S(1)}, u32[]{:S(2)}, u32[]{:S(2)}) async-start(bf16[32,2,1024]{2,1,0:T(2,128)(2,1)} %reshape.372), calls=%async_computation.10 | async-start | bytes 262144 | tf_op jit(solution)/shard_map/all_to_all | solution.py:139
  322.6 0.7 copy.70
  323.7 7.2 %all-to-all-done.10 = bf16[32,2,1024]{2,1,0:T(2,128)(2,1)S(1)} async-done(((bf16[32,2,1024]{2,1,0:T(2,128)(2,1)}), bf16[32,2,1024]{2,1,0:T(2,128)(2,1)S(1)}, u32[]{:S(2)}, u32[]{:S(2)}) %all-to-all-start.10) | async-done | bytes 131104 | tf_op jit(solution)/shard_map/all_to_all | solution.py:139
  332.4 0.7 gather_fusion
  333.1 0.7 gather_fusion.2
  334.5 3.9 %all-to-all-start.11 = ((bf16[32,2,512]{2,1,0:T(2,128)(2,1)}), bf16[32,2,512]{2,1,0:T(2,128)(2,1)S(1)}, u32[]{:S(2)}, u32[]{:S(2)}) async-start(bf16[32,2,512]{2,1,0:T(2,128)(2,1)} %all_to_all.117), calls=%async_computation.11 | async-start | bytes 131072 | tf_op jit(solution)/shard_map/all_to_all | solution.py:148
  339.1 7.7 %all-to-all-done.11 = bf16[32,2,512]{2,1,0:T(2,128)(2,1)S(1)} async-done(((bf16[32,2,512]{2,1,0:T(2,128)(2,1)}), bf16[32,2,512]{2,1,0:T(2,128)(2,1)S(1)}, u32[]{:S(2)}, u32[]{:S(2)}) %all-to-all-start.11) | async-done | bytes 65568 | tf_op jit(solution)/shard_map/all_to_all | solution.py:148
  346.8 3.9 %all-to-all-start.6 = ((bf16[32,2,512]{2,1,0:T(2,128)(2,1)}), bf16[32,2,512]{2,1,0:T(2,128)(2,1)S(1)}, u32[]{:S(2)}, u32[]{:S(2)}) async-start(bf16[32,2,512]{2,1,0:T(2,128)(2,1)} %all_to_all.105), calls=%async_computation.6 | async-start | bytes 131072 | tf_op jit(solution)/shard_map/all_to_all | solution.py:147
  351.3 7.7 %all-to-all-done.6 = bf16[32,2,512]{2,1,0:T(2,128)(2,1)S(1)} async-done(((bf16[32,2,512]{2,1,0:T(2,128)(2,1)}), bf16[32,2,512]{2,1,0:T(2,128)(2,1)S(1)}, u32[]{:S(2)}, u32[]{:S(2)}) %all-to-all-start.6) | async-done | bytes 65568 | tf_op jit(solution)/shard_map/all_to_all | solution.py:147
  359.9 0.9 fusion.4
  360.9 0.9 fusion.5
  (61 shorter events, 12.2 us)
Async XLA Ops:
  0.6 13.3 %copy-start = (bf16[1,32,64,128]{3,2,1,0:T(8,128)(2,1)S(1)}, bf16[1,32,64,128]{3,2,1,0:T(8,128)(2,1)}, u32[]{:S(2)}) copy-start(bf16[1,32,64,128]{3,2,1,0:T(8,128)(2,1)} %param.11) | copy-start | bytes 1572868
  4.5 16.8 %all-to-all-start = ((s32[32,2,1]{1,2,0:T(1,128)}), s32[32,2,1]{1,2,0:T(1,128)S(1)}, u32[]{:S(2)}, u32[]{:S(2)}) async-start(s32[32,2,1]{1,2,0:T(1,128)} %bitcast.5), calls=%async_computation | async-start | bytes 32768 | tf_op jit(solution)/shard_map/all_to_all | solution.py:68
  21.4 12.2 %all-to-all-start.1 = ((bf16[32,2,512]{2,1,0:T(2,128)(2,1)}), bf16[32,2,512]{2,1,0:T(2,128)(2,1)S(1)}, u32[]{:S(2)}, u32[]{:S(2)}) async-start(bf16[32,2,512]{2,1,0:T(2,128)(2,1)} %all_to_all.94), calls=%async_computation.1 | async-start | bytes 131072 | tf_op jit(solution)/shard_map/all_to_all | solution.py:65
  56.1 21.6 %all-to-all-start.2 = ((bf16[32,2,1024]{2,1,0:T(2,128)(2,1)}), bf16[32,2,1024]{2,1,0:T(2,128)(2,1)S(1)}, u32[]{:S(2)}, u32[]{:S(2)}) async-start(bf16[32,2,1024]{2,1,0:T(2,128)(2,1)} %reshape.366), calls=%async_computation.2 | async-start | bytes 262144 | tf_op jit(solution)/shard_map/all_to_all | solution.py:90
  77.7 66.5 %all-to-all-start.7 = ((bf16[32,2,1024]{2,1,0:T(2,128)(2,1)}), bf16[32,2,1024]{2,1,0:T(2,128)(2,1)S(1)}, u32[]{:S(2)}, u32[]{:S(2)}) async-start(bf16[32,2,1024]{2,1,0:T(2,128)(2,1)} %reshape.370), calls=%async_computation.7 | async-start | bytes 262144 | tf_op jit(solution)/shard_map/all_to_all | solution.py:93
  206.9 13.5 %all-to-all-start.3 = ((bf16[16,8,4,128]{3,2,0,1:T(4,128)(2,1)}), bf16[16,8,4,128]{3,2,0,1:T(4,128)(2,1)S(1)}, u32[]{:S(2)}, u32[]{:S(2)}) async-start(bf16[16,8,4,128]{3,2,0,1:T(4,128)(2,1)} %copy.63), calls=%async_computation.3 | async-start | bytes 262144 | tf_op jit(solution)/shard_map/all_to_all | solution.py:106
  220.4 14.7 %all-to-all-start.8 = ((bf16[16,8,4,128]{3,2,0,1:T(4,128)(2,1)}), bf16[16,8,4,128]{3,2,0,1:T(4,128)(2,1)S(1)}, u32[]{:S(2)}, u32[]{:S(2)}) async-start(bf16[16,8,4,128]{3,2,0,1:T(4,128)(2,1)} %copy.77), calls=%async_computation.8 | async-start | bytes 262144 | tf_op jit(solution)/shard_map/all_to_all | solution.py:109
  235.1 12.9 %all-to-all-start.4 = ((bf16[128,1,4,128]{3,2,1,0:T(4,128)(2,1)}), bf16[128,1,4,128]{3,2,1,0:T(4,128)(2,1)S(1)}, u32[]{:S(2)}, u32[]{:S(2)}) async-start(bf16[128,1,4,128]{3,2,1,0:T(4,128)(2,1)} %bitcast.23), calls=%async_computation.4 | async-start | bytes 262144 | tf_op jit(solution)/shard_map/all_to_all | solution.py:122
  248.0 31.4 %all-to-all-start.9 = ((bf16[128,1,4,128]{3,2,1,0:T(4,128)(2,1)}), bf16[128,1,4,128]{3,2,1,0:T(4,128)(2,1)S(1)}, u32[]{:S(2)}, u32[]{:S(2)}) async-start(bf16[128,1,4,128]{3,2,1,0:T(4,128)(2,1)} %bitcast.40), calls=%async_computation.9 | async-start | bytes 262144 | tf_op jit(solution)/shard_map/all_to_all | solution.py:123
  279.4 34.3 %all-to-all-start.5 = ((bf16[32,2,1024]{2,1,0:T(2,128)(2,1)}), bf16[32,2,1024]{2,1,0:T(2,128)(2,1)S(1)}, u32[]{:S(2)}, u32[]{:S(2)}) async-start(bf16[32,2,1024]{2,1,0:T(2,128)(2,1)} %reshape.368), calls=%async_computation.5 | async-start | bytes 262144 | tf_op jit(solution)/shard_map/all_to_all | solution.py:138
  313.7 17.1 %all-to-all-start.10 = ((bf16[32,2,1024]{2,1,0:T(2,128)(2,1)}), bf16[32,2,1024]{2,1,0:T(2,128)(2,1)S(1)}, u32[]{:S(2)}, u32[]{:S(2)}) async-start(bf16[32,2,1024]{2,1,0:T(2,128)(2,1)} %reshape.372), calls=%async_computation.10 | async-start | bytes 262144 | tf_op jit(solution)/shard_map/all_to_all | solution.py:139
  322.1 28.5 %copy-start.1 = (s32[1,32,1]{1,2,0:T(1,128)S(1)}, s32[1,32,1]{1,2,0:T(1,128)}, u32[]{:S(2)}) copy-start(s32[1,32,1]{1,2,0:T(1,128)} %param.12) | copy-start | bytes 388
  334.5 12.2 %all-to-all-start.11 = ((bf16[32,2,512]{2,1,0:T(2,128)(2,1)}), bf16[32,2,512]{2,1,0:T(2,128)(2,1)S(1)}, u32[]{:S(2)}, u32[]{:S(2)}) async-start(bf16[32,2,512]{2,1,0:T(2,128)(2,1)} %all_to_all.117), calls=%async_computation.11 | async-start | bytes 131072 | tf_op jit(solution)/shard_map/all_to_all | solution.py:148
  346.8 12.2 %all-to-all-start.6 = ((bf16[32,2,512]{2,1,0:T(2,128)(2,1)}), bf16[32,2,512]{2,1,0:T(2,128)(2,1)S(1)}, u32[]{:S(2)}, u32[]{:S(2)}) async-start(bf16[32,2,512]{2,1,0:T(2,128)(2,1)} %all_to_all.105), calls=%async_computation.6 | async-start | bytes 131072 | tf_op jit(solution)/shard_map/all_to_all | solution.py:147
where the time goes:
time: 370 us; the launch traced here: 362 us
  local copies, waits for them, and re-layouts  186 us (50%)
  starting transfers between devices  74.5 us (20%)
  waiting for transfers between devices  51.3 us (14%)
  matrix products  36.4 us (10%)
  other arithmetic  11.3 us (3%)
    transpose x3, local copies, waits for them, and re-layouts, to_rows(): shaped.transpose(0, 2, 4, 5, 1, 3)  78.7 us
    transpose x2, local copies, waits for them, and re-layouts, from_rows(): shaped.transpose(0, 4, 1, 5, 2, 3)  28.9 us
    reshape x2, local copies, waits for them, and re-layouts, to_rows(): shaped = grid_part.reshape(slab_x // 4, GY // 4, 4, 4, probe_count, z_piece)  20 us
    reshape x2, local copies, waits for them, and re-layouts, to_rows(): shaped.transpose(0, 2, 4, 5, 1, 3)  17.6 us
    dot_general x1, matrix products, on_device(): slope_z = jnp.dot(z_lines, kz_slope, precision=precise)  14.9 us
    dot_general x1, matrix products, on_device(): along_z = jnp.dot(z_lines, kz_value, precision=precise)  14.9 us
    all_to_all x2, local copies, waits for them, and re-layouts, on_device(): lax.all_to_all(from_rows(value_home), 'pts', split_axis=0, concat_axis=0,...  8.8 us
    all_to_all x2, local copies, waits for them, and re-layouts, on_device(): lax.all_to_all(from_rows(slope_home), 'pts', split_axis=0, concat_axis=0,...  8.8 us
  transfers between devices with their start and end apart: 12, of which 8 were waited for; matrix products, arithmetic and copies ran while one was open for 33% of the time, Pallas kernels for 0%

commit v1 on v0

v1 whole, which is shorter than its diff:
```python
import math

import jax
import jax.numpy as jnp
from jax import lax
from jax.experimental import pallas as pl
from jax.experimental.pallas import tpu as pltpu
from jax.sharding import PartitionSpec as P

EXTENT = 128
ROOT_FIVE = math.sqrt(5.0)
F32 = jnp.float32
BF16 = jnp.bfloat16
I32 = jnp.int32
PEERS = 32


def iota(shape, dim):
    return lax.broadcasted_iota(I32, shape, dim)


def matern(distance, ell):
    scaled = (ROOT_FIVE / EXTENT) * distance / ell
    scale = jnp.exp(-scaled) * lax.rsqrt(EXTENT * ell)
    poly = 1.0 + scaled + scaled * scaled * (1.0 / 3.0)
    value = poly * scale
    slope = (scaled * scaled * (1.0 + scaled) * (1.0 / 3.0) - 0.5 * poly) * scale
    return value, slope


def split(table):
    high = table.astype(BF16)
    low = (table - high.astype(F32)).astype(BF16)
    return high, low


def swapped(place):
    return 4 * (place % 32) + place // 32


def dot(a, b):
    return jnp.dot(a, b, preferred_element_type=F32)


def kernel(
    owner_ref, slot_ref, count_ref, scale_ref, probe_ref, weight_ref, cov_ref, adj_ref,
    sums, sel, lines, field, pieces,
    send1, recv1, send2, recv2, send3, recv3, send4, recv4,
    send_sem, recv_sem,
):
    g = lax.axis_index("grid")
    i = lax.axis_index("pts")
    probe = i // 4
    mine = g * 4 + i % 4

    def pts_peer(k):
        return g, k

    def line_peer(k):
        return k // 4, probe * 4 + k % 4

    barrier = pltpu.get_barrier_semaphore()

    def greet(step, carry):
        for me, peer in ((i, pts_peer), (mine, line_peer)):
            to_g, to_i = peer(lax.rem(me + step, PEERS))
            pl.semaphore_signal(
                barrier, inc=1, device_id={"grid": to_g, "pts": to_i}, device_id_type=pl.DeviceIdType.MESH
            )
        return carry

    lax.fori_loop(1, PEERS, greet, 0)

    def copy(phase, me, peer, source, target, k):
        to_g, to_i = peer(k)
        return pltpu.make_async_remote_copy(
            src_ref=source.at[k],
            dst_ref=target.at[me],
            send_sem=send_sem.at[phase],
            recv_sem=recv_sem.at[phase],
            device_id={"grid": to_g, "pts": to_i},
            device_id_type=pl.DeviceIdType.MESH,
        )

    def start(phase, me, peer, source, target):
        def one(step, carry):
            copy(phase, me, peer, source, target, lax.rem(me + step, PEERS)).start()
            return carry

        lax.fori_loop(1, PEERS, one, 0)
        target[me] = source[me]

    def finish(phase, source, target):
        whole = pltpu.make_async_remote_copy(
            src_ref=source.at[pl.ds(0, PEERS - 1)],
            dst_ref=target.at[pl.ds(0, PEERS - 1)],
            send_sem=send_sem.at[phase],
            recv_sem=recv_sem.at[phase],
            device_id={"grid": g, "pts": i},
            device_id_type=pl.DeviceIdType.MESH,
        )
        whole.wait_send()
        whole.wait_recv()

    ell = jnp.full((1, 1), scale_ref[0], F32)
    lane8 = iota((8, 128), 1)

    used = [jnp.int32(0)] * 4
    lane512 = iota((8, 512), 1)
    probe_row = iota((8, 512), 0) == lane512 // 64
    blocks = probe_ref.shape[0]
    for b in range(blocks):
        owner = owner_ref[0, b]
        slot = slot_ref[0, b]
        column = owner // 8
        rank = jnp.int32(0)
        for c in range(4):
            here = column == c
            rank = jnp.where(here, used[c], rank)
            used[c] = used[c] + here.astype(I32)
        place = column * 16 + rank
        brick_y = (owner % 8) * 4 + slot // 32
        brick_z = slot % 32
        masked = jnp.where(lane8 < count_ref[0, b], probe_ref[b].astype(F32), 0.0).astype(BF16)
        padded = jnp.concatenate([weight_ref[b], jnp.zeros((64, 128), BF16)], axis=0)
        block_sum = lax.dot_general(masked, padded, (((1,), (1,)), ((), ())), preferred_element_type=F32)
        block_sum = jnp.where(lane8 == 64, brick_y.astype(F32), block_sum)
        block_sum = jnp.where(lane8 == 65, brick_z.astype(F32), block_sum)
        sums[pl.ds(b * 8, 8), :] = block_sum
        chosen = probe_row & (lane512 % 64 == place)
        sel[pl.ds(b * 8, 8), :] = chosen.astype(F32)

    spread = sel[...].T.astype(BF16)
    message = dot(spread, sums[...].astype(BF16))
    send1[...] = message.astype(BF16).reshape(PEERS, 16, 128)

    pl.semaphore_wait(barrier, 2 * (PEERS - 1))
    start(0, i, pts_peer, send1, recv1)

    row_z, lane_z = iota((128, 256), 0), iota((128, 256), 1)
    value, slope = matern(jnp.abs(swapped(row_z) - swapped(lane_z % 128)).astype(F32), ell)
    along_z = jnp.concatenate(split(jnp.where(lane_z < 128, value, slope)), axis=0)
    row_y, lane_y = iota((256, 128), 0), iota((256, 128), 1)
    value, slope = matern(jnp.abs(swapped(row_y % 128) - swapped(lane_y)).astype(F32), ell)
    along_y = jnp.concatenate(split(jnp.where(row_y < 128, value, slope)), axis=1)
    row_x, lane_x = iota((256, 256), 0), iota((256, 256), 1)
    x_out = (row_x // 8) * 4 + row_x % 4
    x_in = (lane_x // 8) * 4 + lane_x % 4
    value, slope = matern(jnp.abs(x_out - x_in).astype(F32), ell)
    out_slope = (row_x // 4) % 2
    in_mixed = (lane_x // 4) % 2
    table_x = jnp.where(out_slope == in_mixed, value, jnp.where(out_slope == 1, slope, 0.0))
    along_x = jnp.concatenate(split(table_x), axis=1)

    finish(0, send1, recv1)

    arrived = recv1[...].reshape(PEERS * 16, 128)
    wide = arrived.astype(F32)
    at_y = wide[:, 64:65].astype(I32)
    at_z = wide[:, 65:66].astype(I32)
    lane_s = iota((PEERS * 16, 128), 1)
    is_z = at_z == lane_s % 32
    is_y = (at_y == lane_s).astype(F32)
    is_y_across = is_y.T[0:32].astype(BF16)
    is_y = is_y.astype(BF16)
    cell = iota((128, 256), 0)
    lane = iota((128, 256), 1)
    is_z2 = jnp.concatenate([is_z, is_z], axis=1)
    for t in range(8):
        copies = (cell == t * 8 + lane // 32).astype(F32).astype(BF16)
        placed = jnp.where(is_z2, dot(arrived, copies), 0.0).astype(BF16)
        rows = dot(is_y_across, placed)
        lines[pl.ds(t * 64, 32), :] = rows[:, 0:128]
        lines[pl.ds(t * 64 + 32, 32), :] = rows[:, 128:256]

    cells = lines[...].astype(BF16)
    by_z = dot(jnp.concatenate([cells, cells], axis=1), along_z).astype(BF16)
    for cx in range(4):
        part = by_z[cx * 128 : (cx + 1) * 128]
        by_y = dot(along_y, jnp.concatenate([part, part], axis=0))
        field[pl.ds(cx, 128, stride=8), :] = by_y[0:128, 0:128]
        field[pl.ds(4 + cx, 128, stride=8), :] = by_y[0:128, 128:256] + by_y[128:256, 0:128]
    send2[...] = field[...].astype(BF16).reshape(PEERS, 32, 128)
    start(1, mine, line_peer, send2, recv2)
    finish(1, send2, recv2)

    got = recv2[...].astype(F32)
    for j in range(4):
        part = got[:, j * 8 : (j + 1) * 8, :].reshape(256, 128).astype(BF16)
        by_x = dot(along_x, jnp.concatenate([part, part], axis=0))
        pieces[:, j * 8 : (j + 1) * 8, :] = by_x.reshape(PEERS, 8, 128)
    send3[...] = pieces[...].astype(BF16)
    start(2, mine, line_peer, send3, recv3)
    finish(2, send3, recv3)

    field[...] = recv3[...].astype(F32).reshape(1024, 128)
    is_y32 = is_y[:, 0:32]
    total = jnp.zeros((PEERS * 16, 128), F32)
    row2, lane2 = iota((256, 128), 0), iota((256, 128), 1)
    for t in range(16):
        pair = []
        for u in (2 * t, 2 * t + 1):
            which, cy = u // 4, u % 4
            pair.append(field[pl.ds(cy * 256 + which, 32, stride=8), :])
        rows = jnp.concatenate(pair, axis=1).astype(BF16)
        taken = jnp.where(is_z2, dot(is_y32, rows), 0.0).astype(BF16)
        gather = (lane2 == t * 8 + row2 // 32).astype(F32).astype(BF16)
        total = total + dot(taken, gather)
    send4[...] = total.astype(BF16).reshape(PEERS, 16, 128)
    start(3, i, pts_peer, send4, recv4)
    finish(3, send4, recv4)

    sums[...] = dot(sel[...].astype(BF16), recv4[...].reshape(PEERS * 16, 128))
    for b in range(blocks):
        block = sums[pl.ds(b * 8, 8), :]
        both = jnp.concatenate([jnp.where(lane8 < 64, block, 0.0), jnp.where(lane8 < 64, 0.0, block)], axis=0)
        twice = jnp.concatenate([weight_ref[b], weight_ref[b]], axis=0)
        result = dot(both.astype(BF16), twice)
        usable = lane8 < count_ref[0, b]
        cov_ref[b] = jnp.where(usable, result[0:8], 0.0)
        adj_ref[b] = jnp.where(usable, result[8:16], 0.0)


def on_device(probes, weights, brick_owner, brick_slot, counts, length_scale):
    blocks = probes.shape[1]
    smem = pl.BlockSpec(memory_space=pltpu.SMEM)
    vmem = pl.BlockSpec(memory_space=pltpu.VMEM)
    out = jax.ShapeDtypeStruct((blocks, 8, 128), F32)
    small = pltpu.VMEM((PEERS, 16, 128), BF16)
    large = pltpu.VMEM((PEERS, 32, 128), BF16)
    cov, adj = pl.pallas_call(
        kernel,
        out_shape=(out, out),
        in_specs=[smem, smem, smem, smem, vmem, vmem],
        out_specs=(vmem, vmem),
        scratch_shapes=[
            pltpu.VMEM((256, 128), F32),
            pltpu.VMEM((256, 512), F32),
            pltpu.VMEM((512, 128), F32),
            pltpu.VMEM((1024, 128), F32),
            pltpu.VMEM((PEERS, 32, 128), F32),
            small, small, large, large, large, large, small, small,
            pltpu.SemaphoreType.DMA((4,)),
            pltpu.SemaphoreType.DMA((4,)),
        ],
        compiler_params=pltpu.CompilerParams(collective_id=0, has_side_effects=True),
        name="covariance",
    )(brick_owner.reshape(1, blocks), brick_slot, counts, length_scale, probes[0], weights[0])
    return cov[None], adj[None]


def solution(mesh):
    placed = (
        P("grid", "pts", None, None),
        P("grid", "pts", None, None),
        P("grid", "pts", None),
        P("grid", "pts"),
        P("grid", "pts"),
        P(),
    )
    return jax.shard_map(
        on_device,
        mesh=mesh,
        in_specs=placed,
        out_specs=(P("grid", "pts", None, None), P("grid", "pts", None, None)),
        check_vma=False,
    )
```

time: 370 us -> 49.6 us (0.13)
  the two profiles are of different devices: /device:TPU:64 before, /device:TPU:1 now
where the time goes in v1:
time: 49.6 us; the launch traced here: 49.4 us
  Pallas kernels  45.9 us (93%)
  local copies, waits for them, and re-layouts  2.26 us (5%)
  between operations  1.29 us (3%)
    pallas_call x1, Pallas kernels, on_device(): pl.pallas_call(kernel, out_shape=(out, out), in_specs=[smem, smem, smem,...  45.9 us
    unnamed x4, local copies, waits for them, and re-layouts  2.26 us

profile of v1, /device:TPU:1, one launch (start us, length us, event | category | flops | bytes accessed | tf_op | source)
XLA Modules:
  0.0 49.4 jit_solution(7176562704590124842)
XLA Ops:
  1.3 45.9 %covariance.1 = (f32[32,8,128]{2,1,0:T(8,128)}, f32[32,8,128]{2,1,0:T(8,128)}) custom-call(s32[1,32]{1,0:T(1,128)} %bitcast.9, s32[1,32]{1,0:T(1,128)} %slot_ref.1, s32[1,32]{1,0:T(1,128)} %count_ref.1, f32[1]{0:T(128)S(6)} %copy.10.scale_ref, bf16[32,8,128]{2,1,0:T(8,128)(2,1)} %bitcast.8, bf16[32,64,128]{2,1,0:T(8,128)(2,1)} %bitcast.5), custom_call_target="tpu_custom_call" | custom-call | tf_op jit(solution)/shard_map/covariance/pallas_call | solution.py:231
  47.2 0.0 copy-start
  47.2 1.6 %copy.11 = f32[1,32,8,128]{3,2,1,0:T(8,128)} copy(f32[1,32,8,128]{3,2,1,0:T(8,128)} %bitcast.7) | data formatting | bytes 262144
  48.8 0.0 copy-done
  48.8 0.7 %copy.12 = f32[1,32,8,128]{3,2,1,0:T(8,128)} copy(f32[1,32,8,128]{3,2,1,0:T(8,128)S(1)} %bitcast.6) | data formatting | bytes 262144
Async XLA Ops:
  47.2 1.6 %copy-start = (f32[32,8,128]{2,1,0:T(8,128)S(1)}, f32[32,8,128]{2,1,0:T(8,128)}, u32[]{:S(2)}) copy-start(f32[32,8,128]{2,1,0:T(8,128)} %get-tuple-element.5) | copy-start | bytes 393220

commit v2 on v1

--- a/solution.py
+++ b/solution.py
@@ -1,3 +1,4 @@
+import functools
 import math
 
 import jax
@@ -43,8 +44,8 @@
 
 
 def kernel(
-    owner_ref, slot_ref, count_ref, scale_ref, probe_ref, weight_ref, cov_ref, adj_ref,
-    sums, sel, lines, field, pieces,
+    chunks, owner_ref, slot_ref, count_ref, scale_ref, probe_ref, weight_ref, rows_ref,
+    sums, sel, lines, field, total,
     send1, recv1, send2, recv2, send3, recv3, send4, recv4,
     send_sem, recv_sem,
 ):
@@ -52,55 +53,58 @@
     i = lax.axis_index("pts")
     probe = i // 4
     mine = g * 4 + i % 4
-
-    def pts_peer(k):
-        return g, k
-
-    def line_peer(k):
-        return k // 4, probe * 4 + k % 4
+    at_z, core = (g // 2) * 2 + i % 2, g % 2
+    per = 4 // chunks
+
+    def hops(shift, size):
+        return min(shift, size - shift)
+
+    def farthest(sizes):
+        shifts = [()]
+        for size in sizes:
+            shifts = [old + (new,) for old in shifts for new in range(size)]
+        return shifts
+
+    pts_shifts = sorted(farthest((4, 4, 2))[1:], key=lambda s: -hops(s[0], 4) - hops(s[1], 4) - s[2])
+    line_shifts = sorted(farthest((8, 2, 2))[1:], key=lambda s: -hops(s[0], 8) - s[1] - 0.1 * s[2])
+
+    def pts_peer(shift):
+        to = lax.rem(i // 8 + shift[0], 4) * 8 + lax.rem(i // 2 % 4 + shift[1], 4) * 2 + lax.rem(i % 2 + shift[2], 2)
+        return to, {"grid": g, "pts": to}
+
+    def line_peer(shift):
+        z = lax.rem(at_z + shift[0], 8)
+        place = lax.rem(i // 2 % 2 + shift[1], 2) * 2 + z % 2
+        to_g = (z // 2) * 2 + lax.rem(core + shift[2], 2)
+        return to_g * 4 + place, {"grid": to_g, "pts": probe * 4 + place}
 
     barrier = pltpu.get_barrier_semaphore()
-
-    def greet(step, carry):
-        for me, peer in ((i, pts_peer), (mine, line_peer)):
-            to_g, to_i = peer(lax.rem(me + step, PEERS))
-            pl.semaphore_signal(
-                barrier, inc=1, device_id={"grid": to_g, "pts": to_i}, device_id_type=pl.DeviceIdType.MESH
-            )
-        return carry
-
-    lax.fori_loop(1, PEERS, greet, 0)
-
-    def copy(phase, me, peer, source, target, k):
-        to_g, to_i = peer(k)
+    for peer, shifts in ((line_peer, line_shifts), (pts_peer, pts_shifts)):
+        for shift in shifts:
+            pl.semaphore_signal(barrier, inc=1, device_id=peer(shift)[1], device_id_type=pl.DeviceIdType.MESH)
+
+    def start(sem, me, peer, shifts, source, target):
+        for shift in shifts:
+            k, device = peer(shift)
+            pltpu.make_async_remote_copy(
+                src_ref=source.at[k],
+                dst_ref=target.at[me],
+                send_sem=send_sem.at[sem],
+                recv_sem=recv_sem.at[sem],
+                device_id=device,
+                device_id_type=pl.DeviceIdType.MESH,
+            ).start()
+        target[me] = source[me]
+
+    def whole(sem, source, target):
         return pltpu.make_async_remote_copy(
-            src_ref=source.at[k],
-            dst_ref=target.at[me],
-            send_sem=send_sem.at[phase],
-            recv_sem=recv_sem.at[phase],
-            device_id={"grid": to_g, "pts": to_i},
-            device_id_type=pl.DeviceIdType.MESH,
-        )
-
-    def start(phase, me, peer, source, target):
-        def one(step, carry):
-            copy(phase, me, peer, source, target, lax.rem(me + step, PEERS)).start()
-            return carry
-
-        lax.fori_loop(1, PEERS, one, 0)
-        target[me] = source[me]
-
-    def finish(phase, source, target):
-        whole = pltpu.make_async_remote_copy(
             src_ref=source.at[pl.ds(0, PEERS - 1)],
             dst_ref=target.at[pl.ds(0, PEERS - 1)],
-            send_sem=send_sem.at[phase],
-            recv_sem=recv_sem.at[phase],
+            send_sem=send_sem.at[sem],
+            recv_sem=recv_sem.at[sem],
             device_id={"grid": g, "pts": i},
             device_id_type=pl.DeviceIdType.MESH,
         )
-        whole.wait_send()
-        whole.wait_recv()
 
     ell = jnp.full((1, 1), scale_ref[0], F32)
     lane8 = iota((8, 128), 1)
@@ -135,7 +139,7 @@
     send1[...] = message.astype(BF16).reshape(PEERS, 16, 128)
 
     pl.semaphore_wait(barrier, 2 * (PEERS - 1))
-    start(0, i, pts_peer, send1, recv1)
+    start(0, i, pts_peer, pts_shifts, send1, recv1)
 
     row_z, lane_z = iota((128, 256), 0), iota((128, 256), 1)
     value, slope = matern(jnp.abs(swapped(row_z) - swapped(lane_z % 128)).astype(F32), ell)
@@ -152,15 +156,15 @@
     table_x = jnp.where(out_slope == in_mixed, value, jnp.where(out_slope == 1, slope, 0.0))
     along_x = jnp.concatenate(split(table_x), axis=1)
 
-    finish(0, send1, recv1)
+    whole(0, send1, recv1).wait_recv()
 
     arrived = recv1[...].reshape(PEERS * 16, 128)
     wide = arrived.astype(F32)
-    at_y = wide[:, 64:65].astype(I32)
-    at_z = wide[:, 65:66].astype(I32)
+    brick_y = wide[:, 64:65].astype(I32)
+    brick_z = wide[:, 65:66].astype(I32)
     lane_s = iota((PEERS * 16, 128), 1)
-    is_z = at_z == lane_s % 32
-    is_y = (at_y == lane_s).astype(F32)
+    is_z = brick_z == lane_s % 32
+    is_y = (brick_y == lane_s).astype(F32)
     is_y_across = is_y.T[0:32].astype(BF16)
     is_y = is_y.astype(BF16)
     cell = iota((128, 256), 0)
@@ -180,39 +184,55 @@
         by_y = dot(along_y, jnp.concatenate([part, part], axis=0))
         field[pl.ds(cx, 128, stride=8), :] = by_y[0:128, 0:128]
         field[pl.ds(4 + cx, 128, stride=8), :] = by_y[0:128, 128:256] + by_y[128:256, 0:128]
-    send2[...] = field[...].astype(BF16).reshape(PEERS, 32, 128)
-    start(1, mine, line_peer, send2, recv2)
-    finish(1, send2, recv2)
-
-    got = recv2[...].astype(F32)
-    for j in range(4):
-        part = got[:, j * 8 : (j + 1) * 8, :].reshape(256, 128).astype(BF16)
-        by_x = dot(along_x, jnp.concatenate([part, part], axis=0))
-        pieces[:, j * 8 : (j + 1) * 8, :] = by_x.reshape(PEERS, 8, 128)
-    send3[...] = pieces[...].astype(BF16)
-    start(2, mine, line_peer, send3, recv3)
-    finish(2, send3, recv3)
-
-    field[...] = recv3[...].astype(F32).reshape(1024, 128)
+    for c in range(chunks):
+        for k in range(per):
+            cy = c * per + k
+            send2[c, :, k] = field[pl.ds(cy * 256, 256), :].reshape(PEERS, 8, 128).astype(BF16)
+        start(1 + c, mine, line_peer, line_shifts, send2.at[c], recv2.at[c])
+
+    for c in range(chunks):
+        whole(1 + c, send2.at[c], recv2.at[c]).wait_recv()
+        for k in range(per):
+            part = recv2[c, :, k].astype(F32).reshape(256, 128).astype(BF16)
+            by_x = dot(along_x, jnp.concatenate([part, part], axis=0))
+            send3[c, :, k] = by_x.reshape(PEERS, 8, 128).astype(BF16)
+        start(1 + chunks + c, mine, line_peer, line_shifts, send3.at[c], recv3.at[c])
+
     is_y32 = is_y[:, 0:32]
-    total = jnp.zeros((PEERS * 16, 128), F32)
     row2, lane2 = iota((256, 128), 0), iota((256, 128), 1)
-    for t in range(16):
-        pair = []
-        for u in (2 * t, 2 * t + 1):
-            which, cy = u // 4, u % 4
-            pair.append(field[pl.ds(cy * 256 + which, 32, stride=8), :])
-        rows = jnp.concatenate(pair, axis=1).astype(BF16)
-        taken = jnp.where(is_z2, dot(is_y32, rows), 0.0).astype(BF16)
-        gather = (lane2 == t * 8 + row2 // 32).astype(F32).astype(BF16)
-        total = total + dot(taken, gather)
-    send4[...] = total.astype(BF16).reshape(PEERS, 16, 128)
-    start(3, i, pts_peer, send4, recv4)
-    finish(3, send4, recv4)
-
-    sums[...] = dot(sel[...].astype(BF16), recv4[...].reshape(PEERS * 16, 128))
-    for b in range(blocks):
-        block = sums[pl.ds(b * 8, 8), :]
+    for c in range(chunks):
+        whole(1 + chunks + c, send3.at[c], recv3.at[c]).wait_recv()
+        for k in range(per):
+            cy = c * per + k
+            field[pl.ds(cy * 256, 256), :] = recv3[c, :, k].astype(F32).reshape(256, 128)
+            gathered = jnp.zeros((PEERS * 16, 128), F32)
+            for w in (0, 2, 4, 6):
+                pair = [field[pl.ds(cy * 256 + w + u, 32, stride=8), :] for u in range(2)]
+                rows = jnp.concatenate(pair, axis=1).astype(BF16)
+                taken = jnp.where(is_z2, dot(is_y32, rows), 0.0).astype(BF16)
+                cell_of = (w + row2 // 128) * 16 + cy * 4 + row2 % 128 // 32
+                gathered = gathered + dot(taken, (lane2 == cell_of).astype(F32).astype(BF16))
+            if cy == 0:
+                total[...] = gathered
+            elif cy < 3:
+                total[...] = total[...] + gathered
+            else:
+                send4[...] = (total[...] + gathered).astype(BF16).reshape(PEERS, 16, 128)
+    last = 1 + 2 * chunks
+    start(last, i, pts_peer, pts_shifts, send4, recv4)
+    whole(0, send1, recv1).wait_send()
+    for c in range(chunks):
+        whole(1 + c, send2.at[c], recv2.at[c]).wait_send()
+        whole(1 + chunks + c, send3.at[c], recv3.at[c]).wait_send()
+    whole(last, send4, recv4).wait_recv()
+    rows_ref[...] = dot(sel[...].astype(BF16), recv4[...].reshape(PEERS * 16, 128))
+    whole(last, send4, recv4).wait_send()
+
+
+def points_kernel(count_ref, rows_ref, weight_ref, cov_ref, adj_ref):
+    lane8 = iota((8, 128), 1)
+    for b in range(weight_ref.shape[0]):
+        block = rows_ref[pl.ds(b * 8, 8), :]
         both = jnp.concatenate([jnp.where(lane8 < 64, block, 0.0), jnp.where(lane8 < 64, 0.0, block)], axis=0)
         twice = jnp.concatenate([weight_ref[b], weight_ref[b]], axis=0)
         result = dot(both.astype(BF16), twice)
@@ -221,31 +241,42 @@
         adj_ref[b] = jnp.where(usable, result[8:16], 0.0)
 
 
+CHUNKS = 4
+
+
 def on_device(probes, weights, brick_owner, brick_slot, counts, length_scale):
     blocks = probes.shape[1]
+    chunks = CHUNKS
     smem = pl.BlockSpec(memory_space=pltpu.SMEM)
     vmem = pl.BlockSpec(memory_space=pltpu.VMEM)
-    out = jax.ShapeDtypeStruct((blocks, 8, 128), F32)
     small = pltpu.VMEM((PEERS, 16, 128), BF16)
-    large = pltpu.VMEM((PEERS, 32, 128), BF16)
-    cov, adj = pl.pallas_call(
-        kernel,
-        out_shape=(out, out),
+    large = pltpu.VMEM((chunks, PEERS, 4 // chunks, 8, 128), BF16)
+    rows = pl.pallas_call(
+        functools.partial(kernel, chunks),
+        out_shape=jax.ShapeDtypeStruct((blocks * 8, 128), F32),
         in_specs=[smem, smem, smem, smem, vmem, vmem],
-        out_specs=(vmem, vmem),
+        out_specs=vmem,
         scratch_shapes=[
             pltpu.VMEM((256, 128), F32),
             pltpu.VMEM((256, 512), F32),
             pltpu.VMEM((512, 128), F32),
             pltpu.VMEM((1024, 128), F32),
-            pltpu.VMEM((PEERS, 32, 128), F32),
+            pltpu.VMEM((512, 128), F32),
             small, small, large, large, large, large, small, small,
-            pltpu.SemaphoreType.DMA((4,)),
-            pltpu.SemaphoreType.DMA((4,)),
+            pltpu.SemaphoreType.DMA((2 + 2 * chunks,)),
+            pltpu.SemaphoreType.DMA((2 + 2 * chunks,)),
         ],
         compiler_params=pltpu.CompilerParams(collective_id=0, has_side_effects=True),
         name="covariance",
     )(brick_owner.reshape(1, blocks), brick_slot, counts, length_scale, probes[0], weights[0])
+    out = jax.ShapeDtypeStruct((blocks, 8, 128), F32)
+    cov, adj = pl.pallas_call(
+        points_kernel,
+        out_shape=(out, out),
+        in_specs=[smem, vmem, vmem],
+        out_specs=(vmem, vmem),
+        name="points",
+    )(counts, rows, weights[0])
     return cov[None], adj[None]
 
 

time: 49.6 us -> 44.5 us (0.90)
  Pallas kernels: 45.9 us -> 43.1 us
  local copies, waits for them, and re-layouts: 2.26 us -> 0 us
    pallas_call x1 -> x2, Pallas kernels: 45.9 us -> 43.1 us  [the longest x1 40.9 us: on_device(): pl.pallas_call(functools.partial(kernel, chunks), out_shape=jax.ShapeDtyp...]
    unnamed x4 -> x0, local copies, waits for them, and re-layouts: 2.26 us -> none
where the time goes in v2:
time: 44.5 us; the launch traced here: 44.4 us
  Pallas kernels  43.1 us (97%)
  between operations  1.29 us (3%)
    pallas_call x1, Pallas kernels, on_device(): pl.pallas_call(functools.partial(kernel, chunks), out_shape=jax.ShapeDtyp...  40.9 us
    pallas_call x1, Pallas kernels, on_device(): pl.pallas_call(points_kernel, out_shape=(out, out), in_specs=[smem, vmem,...  2.21 us

profile of v2, /device:TPU:1, one launch (start us, length us, event | category | flops | bytes accessed | tf_op | source)
XLA Modules:
  0.0 44.4 jit_solution(9492687358104012489)
XLA Ops:
  1.3 40.9 %covariance.1.rows_ref = f32[256,128]{1,0:T(8,128)} custom-call(s32[1,32]{1,0:T(1,128)} %bitcast.8, s32[1,32]{1,0:T(1,128)} %slot_ref.1, s32[1,32]{1,0:T(1,128)} %count_ref.3, f32[1]{0:T(128)S(6)} %copy.8.scale_ref, bf16[32,8,128]{2,1,0:T(8,128)(2,1)} %bitcast.7, bf16[32,64,128]{2,1,0:T(8,128)(2,1)} %bitcast.5), custom_call_target="tpu_custom_call" | custom-call | tf_op jit(solution)/shard_map/covariance/pallas_call | solution.py:254
  42.2 2.2 %points.1 = (f32[32,8,128]{2,1,0:T(8,128)}, f32[32,8,128]{2,1,0:T(8,128)}) custom-call(s32[1,32]{1,0:T(1,128)} %count_ref.3, f32[256,128]{1,0:T(8,128)} %covariance.1.rows_ref, bf16[32,64,128]{2,1,0:T(8,128)(2,1)} %bitcast.6), custom_call_target="tpu_custom_call" | custom-call | tf_op jit(solution)/shard_map/points/pallas_call | solution.py:273

commit v3 on v2

--- a/solution.py
+++ b/solution.py
@@ -44,10 +44,10 @@
 
 
 def kernel(
-    chunks, owner_ref, slot_ref, count_ref, scale_ref, probe_ref, weight_ref, rows_ref,
-    sums, sel, lines, field, total,
+    chunks, owner_hbm, slot_hbm, count_hbm, probe_hbm, weight_hbm, scale_hbm, rows_ref,
+    owner_ref, slot_ref, count_ref, scale_ref, probe_ref, weight_ref, sums, sel, lines, field, total,
     send1, recv1, send2, recv2, send3, recv3, send4, recv4,
-    send_sem, recv_sem,
+    send_sem, recv_sem, load_sem,
 ):
     g = lax.axis_index("grid")
     i = lax.axis_index("pts")
@@ -82,6 +82,18 @@
     for peer, shifts in ((line_peer, line_shifts), (pts_peer, pts_shifts)):
         for shift in shifts:
             pl.semaphore_signal(barrier, inc=1, device_id=peer(shift)[1], device_id_type=pl.DeviceIdType.MESH)
+
+    loads = [
+        pltpu.make_async_copy(source, target, load_sem.at[n])
+        for n, (source, target) in enumerate(
+            (
+                (owner_hbm, owner_ref), (slot_hbm, slot_ref), (count_hbm, count_ref),
+                (probe_hbm, probe_ref), (weight_hbm, weight_ref), (scale_hbm, scale_ref),
+            )
+        )
+    ]
+    for load in loads:
+        load.start()
 
     def start(sem, me, peer, shifts, source, target):
         for shift in shifts:
@@ -106,6 +118,8 @@
             device_id_type=pl.DeviceIdType.MESH,
         )
 
+    for load in loads:
+        load.wait()
     ell = jnp.full((1, 1), scale_ref[0], F32)
     lane8 = iota((8, 128), 1)
 
@@ -254,9 +268,15 @@
     rows = pl.pallas_call(
         functools.partial(kernel, chunks),
         out_shape=jax.ShapeDtypeStruct((blocks * 8, 128), F32),
-        in_specs=[smem, smem, smem, smem, vmem, vmem],
+        in_specs=[pl.BlockSpec(memory_space=pl.ANY)] * 6,
         out_specs=vmem,
         scratch_shapes=[
+            pltpu.SMEM((1, blocks), I32),
+            pltpu.SMEM((1, blocks), I32),
+            pltpu.SMEM((1, blocks), I32),
+            pltpu.SMEM((1,), F32),
+            pltpu.VMEM(probes.shape[1:], BF16),
+            pltpu.VMEM(weights.shape[1:], BF16),
             pltpu.VMEM((256, 128), F32),
             pltpu.VMEM((256, 512), F32),
             pltpu.VMEM((512, 128), F32),
@@ -265,16 +285,24 @@
             small, small, large, large, large, large, small, small,
             pltpu.SemaphoreType.DMA((2 + 2 * chunks,)),
             pltpu.SemaphoreType.DMA((2 + 2 * chunks,)),
+            pltpu.SemaphoreType.DMA((6,)),
         ],
-        compiler_params=pltpu.CompilerParams(collective_id=0, has_side_effects=True),
+        compiler_params=pltpu.CompilerParams(collective_id=0, has_side_effects=True, vmem_limit_bytes=24 << 20),
         name="covariance",
-    )(brick_owner.reshape(1, blocks), brick_slot, counts, length_scale, probes[0], weights[0])
+    )(
+        *(
+            pltpu.with_memory_space_constraint(a, pltpu.HBM)
+            for a in (brick_owner.reshape(1, blocks), brick_slot, counts, probes[0], weights[0])
+        ),
+        length_scale,
+    )
     out = jax.ShapeDtypeStruct((blocks, 8, 128), F32)
     cov, adj = pl.pallas_call(
         points_kernel,
         out_shape=(out, out),
         in_specs=[smem, vmem, vmem],
         out_specs=(vmem, vmem),
+        compiler_params=pltpu.CompilerParams(vmem_limit_bytes=16 << 20),
         name="points",
     )(counts, rows, weights[0])
     return cov[None], adj[None]

time: 44.5 us -> 42.2 us (0.948)
  Pallas kernels: 43.1 us -> 40.7 us
    pallas_call x1, Pallas kernels: 40.9 us -> 39.1 us  [on_device(): pl.pallas_call(functools.partial(kernel, chunks), out_shape=jax.ShapeDtyp...]
    pallas_call x1, Pallas kernels: 2.21 us -> 1.63 us  [on_device(): pl.pallas_call(points_kernel, out_shape=(out, out), in_specs=[smem, vmem,...]
where the time goes in v3:
time: 42.2 us; the launch traced here: 42.1 us
  Pallas kernels  40.7 us (96%)
  between operations  1.37 us (3%)
    pallas_call x1, Pallas kernels, on_device(): pl.pallas_call(functools.partial(kernel, chunks), out_shape=jax.ShapeDtyp...  39.1 us
    pallas_call x1, Pallas kernels, on_device(): pl.pallas_call(points_kernel, out_shape=(out, out), in_specs=[smem, vmem,...  1.63 us

profile of v3, /device:TPU:1, one launch (start us, length us, event | category | flops | bytes accessed | tf_op | source)
XLA Modules:
  0.0 42.1 jit_solution(14039011935947883489)
XLA Ops:
  0.6 0.0 copy-start
  1.3 0.0 copy-start.1
  1.4 39.1 %covariance.1.rows_ref = f32[256,128]{1,0:T(8,128)S(1)} custom-call(s32[1,32]{1,0:T(1,128)} %bitcast.8, s32[1,32]{1,0:T(1,128)} %slot_hbm.1, s32[1,32]{1,0:T(1,128)} %count_ref.1, bf16[32,8,128]{2,1,0:T(8,128)(2,1)} %bitcast.7, bf16[32,64,128]{2,1,0:T(8,128)(2,1)} %bitcast.5, f32[1]{0:T(128)S(6)} %copy.8.scale_hbm), custom_call_target="tpu_custom_call" | custom-call | tf_op jit(solution)/shard_map/covariance/pallas_call | solution.py:268
  40.5 0.0 copy-done
  40.5 0.0 copy-done.1
  40.5 1.6 %points.1 = (f32[32,8,128]{2,1,0:T(8,128)}, f32[32,8,128]{2,1,0:T(8,128)}) custom-call(s32[1,32]{1,0:T(1,128)S(1)} %copy-done.1, f32[256,128]{1,0:T(8,128)S(1)} %covariance.1.rows_ref, bf16[32,64,128]{2,1,0:T(8,128)(2,1)S(1)} %bitcast.6), custom_call_target="tpu_custom_call" | custom-call | tf_op jit(solution)/shard_map/points/pallas_call | solution.py:300
Async XLA Ops:
  0.6 39.8 %copy-start = (bf16[1,32,64,128]{3,2,1,0:T(8,128)(2,1)S(1)}, bf16[1,32,64,128]{3,2,1,0:T(8,128)(2,1)}, u32[]{:S(2)}) copy-start(bf16[1,32,64,128]{3,2,1,0:T(8,128)(2,1)} %param.7) | copy-start | bytes 1572868
  1.3 39.1 %copy-start.1 = (s32[1,32]{1,0:T(1,128)S(1)}, s32[1,32]{1,0:T(1,128)}, u32[]{:S(2)}) copy-start(s32[1,32]{1,0:T(1,128)} %count_ref.1) | copy-start | bytes 388

commit v4 on v3

--- a/solution.py
+++ b/solution.py
@@ -44,8 +44,8 @@
 
 
 def kernel(
-    chunks, owner_hbm, slot_hbm, count_hbm, probe_hbm, weight_hbm, scale_hbm, rows_ref,
-    owner_ref, slot_ref, count_ref, scale_ref, probe_ref, weight_ref, sums, sel, lines, field, total,
+    chunks, owner_hbm, slot_hbm, count_hbm, probe_hbm, weight_hbm, scale_hbm, rows_ref, usable_ref,
+    owner_ref, slot_ref, count_ref, scale_ref, probe_ref, weight_ref, sums, sel, slots, placed, lines, field, gather, total,
     send1, recv1, send2, recv2, send3, recv3, send4, recv4,
     send_sem, recv_sem, load_sem,
 ):
@@ -120,7 +120,7 @@
 
     for load in loads:
         load.wait()
-    ell = jnp.full((1, 1), scale_ref[0], F32)
+    ell = jnp.full((1, 1), scale_ref[0, 0], F32)
     lane8 = iota((8, 128), 1)
 
     used = [jnp.int32(0)] * 4
@@ -139,7 +139,9 @@
         place = column * 16 + rank
         brick_y = (owner % 8) * 4 + slot // 32
         brick_z = slot % 32
-        masked = jnp.where(lane8 < count_ref[0, b], probe_ref[b].astype(F32), 0.0).astype(BF16)
+        usable = lane8 < count_ref[0, b]
+        usable_ref[b] = usable.astype(F32)
+        masked = jnp.where(usable, probe_ref[b].astype(F32), 0.0).astype(BF16)
         padded = jnp.concatenate([weight_ref[b], jnp.zeros((64, 128), BF16)], axis=0)
         block_sum = lax.dot_general(masked, padded, (((1,), (1,)), ((), ())), preferred_element_type=F32)
         block_sum = jnp.where(lane8 == 64, brick_y.astype(F32), block_sum)
@@ -172,24 +174,26 @@
 
     whole(0, send1, recv1).wait_recv()
 
-    arrived = recv1[...].reshape(PEERS * 16, 128)
-    wide = arrived.astype(F32)
+    wide = recv1[...].reshape(PEERS * 16, 128).astype(F32)
     brick_y = wide[:, 64:65].astype(I32)
     brick_z = wide[:, 65:66].astype(I32)
-    lane_s = iota((PEERS * 16, 128), 1)
-    is_z = brick_z == lane_s % 32
-    is_y = (brick_y == lane_s).astype(F32)
-    is_y_across = is_y.T[0:32].astype(BF16)
-    is_y = is_y.astype(BF16)
-    cell = iota((128, 256), 0)
-    lane = iota((128, 256), 1)
-    is_z2 = jnp.concatenate([is_z, is_z], axis=1)
+    across = wide.T[0:64].astype(BF16)
+    lane256 = iota((PEERS * 16, 256), 1)
+    brick = brick_y * 32 + brick_z
+    for t in range(4):
+        there = (lane256 == brick - t * 256).astype(F32).astype(BF16)
+        cells = dot(across, there)
+        placed[pl.ds(t * 128, 64), :] = cells[:, 0:128]
+        placed[pl.ds(t * 128 + 64, 64), :] = cells[:, 128:256]
+    group = iota((16, 128), 1) // 32
     for t in range(8):
-        copies = (cell == t * 8 + lane // 32).astype(F32).astype(BF16)
-        placed = jnp.where(is_z2, dot(arrived, copies), 0.0).astype(BF16)
-        rows = dot(is_y_across, placed)
-        lines[pl.ds(t * 64, 32), :] = rows[:, 0:128]
-        lines[pl.ds(t * 64 + 32, 32), :] = rows[:, 128:256]
+        parts = [placed[pl.ds(t * 64 + cz, 16, stride=4), :] for cz in range(4)]
+        for u in range(4):
+            turned = [parts[cz] if cz == u else pltpu.roll(parts[cz], (cz - u) % 4 * 32, 1) for cz in range(4)]
+            row = jnp.where(
+                group < 2, jnp.where(group == 0, turned[0], turned[1]), jnp.where(group == 2, turned[2], turned[3])
+            )
+            lines[pl.ds(t * 4 + u, 16, stride=32), :] = row
 
     cells = lines[...].astype(BF16)
     by_z = dot(jnp.concatenate([cells, cells], axis=1), along_z).astype(BF16)
@@ -204,6 +208,15 @@
             send2[c, :, k] = field[pl.ds(cy * 256, 256), :].reshape(PEERS, 8, 128).astype(BF16)
         start(1 + c, mine, line_peer, line_shifts, send2.at[c], recv2.at[c])
 
+    lane_s = iota((PEERS * 16, 128), 1)
+    is_z = brick_z == lane_s % 32
+    is_y32 = (brick_y == lane_s).astype(F32).astype(BF16)[:, 0:32]
+    is_z2 = jnp.concatenate([is_z, is_z], axis=1)
+    place, lane = iota((1024, 128), 0), iota((1024, 128), 1)
+    for cy in range(4):
+        gather[cy] = (lane == place // 128 * 16 + cy * 4 + place % 128 // 32).astype(F32).astype(BF16)
+    slots[...] = sel[...].astype(BF16)
+
     for c in range(chunks):
         whole(1 + c, send2.at[c], recv2.at[c]).wait_recv()
         for k in range(per):
@@ -212,20 +225,17 @@
             send3[c, :, k] = by_x.reshape(PEERS, 8, 128).astype(BF16)
         start(1 + chunks + c, mine, line_peer, line_shifts, send3.at[c], recv3.at[c])
 
-    is_y32 = is_y[:, 0:32]
-    row2, lane2 = iota((256, 128), 0), iota((256, 128), 1)
     for c in range(chunks):
         whole(1 + chunks + c, send3.at[c], recv3.at[c]).wait_recv()
         for k in range(per):
             cy = c * per + k
             field[pl.ds(cy * 256, 256), :] = recv3[c, :, k].astype(F32).reshape(256, 128)
-            gathered = jnp.zeros((PEERS * 16, 128), F32)
+            taken = []
             for w in (0, 2, 4, 6):
                 pair = [field[pl.ds(cy * 256 + w + u, 32, stride=8), :] for u in range(2)]
                 rows = jnp.concatenate(pair, axis=1).astype(BF16)
-                taken = jnp.where(is_z2, dot(is_y32, rows), 0.0).astype(BF16)
-                cell_of = (w + row2 // 128) * 16 + cy * 4 + row2 % 128 // 32
-                gathered = gathered + dot(taken, (lane2 == cell_of).astype(F32).astype(BF16))
+                taken.append(jnp.where(is_z2, dot(is_y32, rows), 0.0).astype(BF16))
+            gathered = dot(jnp.concatenate(taken, axis=1), gather[cy])
             if cy == 0:
                 total[...] = gathered
             elif cy < 3:
@@ -239,18 +249,18 @@
         whole(1 + c, send2.at[c], recv2.at[c]).wait_send()
         whole(1 + chunks + c, send3.at[c], recv3.at[c]).wait_send()
     whole(last, send4, recv4).wait_recv()
-    rows_ref[...] = dot(sel[...].astype(BF16), recv4[...].reshape(PEERS * 16, 128))
+    rows_ref[...] = dot(slots[...], recv4[...].reshape(PEERS * 16, 128))
     whole(last, send4, recv4).wait_send()
 
 
-def points_kernel(count_ref, rows_ref, weight_ref, cov_ref, adj_ref):
+def points_kernel(usable_ref, rows_ref, weight_ref, cov_ref, adj_ref):
     lane8 = iota((8, 128), 1)
     for b in range(weight_ref.shape[0]):
         block = rows_ref[pl.ds(b * 8, 8), :]
         both = jnp.concatenate([jnp.where(lane8 < 64, block, 0.0), jnp.where(lane8 < 64, 0.0, block)], axis=0)
         twice = jnp.concatenate([weight_ref[b], weight_ref[b]], axis=0)
         result = dot(both.astype(BF16), twice)
-        usable = lane8 < count_ref[0, b]
+        usable = usable_ref[b] > 0.0
         cov_ref[b] = jnp.where(usable, result[0:8], 0.0)
         adj_ref[b] = jnp.where(usable, result[8:16], 0.0)
 
@@ -261,26 +271,28 @@
 def on_device(probes, weights, brick_owner, brick_slot, counts, length_scale):
     blocks = probes.shape[1]
     chunks = CHUNKS
-    smem = pl.BlockSpec(memory_space=pltpu.SMEM)
     vmem = pl.BlockSpec(memory_space=pltpu.VMEM)
     small = pltpu.VMEM((PEERS, 16, 128), BF16)
     large = pltpu.VMEM((chunks, PEERS, 4 // chunks, 8, 128), BF16)
-    rows = pl.pallas_call(
+    rows, usable = pl.pallas_call(
         functools.partial(kernel, chunks),
-        out_shape=jax.ShapeDtypeStruct((blocks * 8, 128), F32),
+        out_shape=(jax.ShapeDtypeStruct((blocks * 8, 128), F32), jax.ShapeDtypeStruct((blocks, 8, 128), F32)),
         in_specs=[pl.BlockSpec(memory_space=pl.ANY)] * 6,
-        out_specs=vmem,
+        out_specs=(vmem, vmem),
         scratch_shapes=[
             pltpu.SMEM((1, blocks), I32),
             pltpu.SMEM((1, blocks), I32),
             pltpu.SMEM((1, blocks), I32),
-            pltpu.SMEM((1,), F32),
+            pltpu.SMEM((1, 1), F32),
             pltpu.VMEM(probes.shape[1:], BF16),
             pltpu.VMEM(weights.shape[1:], BF16),
             pltpu.VMEM((256, 128), F32),
             pltpu.VMEM((256, 512), F32),
+            pltpu.VMEM((256, 512), BF16),
+            pltpu.VMEM((512, 128), F32),
             pltpu.VMEM((512, 128), F32),
             pltpu.VMEM((1024, 128), F32),
+            pltpu.VMEM((4, 1024, 128), BF16),
             pltpu.VMEM((512, 128), F32),
             small, small, large, large, large, large, small, small,
             pltpu.SemaphoreType.DMA((2 + 2 * chunks,)),
@@ -300,11 +312,11 @@
     cov, adj = pl.pallas_call(
         points_kernel,
         out_shape=(out, out),
-        in_specs=[smem, vmem, vmem],
+        in_specs=[vmem, vmem, vmem],
         out_specs=(vmem, vmem),
         compiler_params=pltpu.CompilerParams(vmem_limit_bytes=16 << 20),
         name="points",
-    )(counts, rows, weights[0])
+    )(usable, rows, weights[0])
     return cov[None], adj[None]
 
 
@@ -315,12 +327,18 @@
         P("grid", "pts", None),
         P("grid", "pts"),
         P("grid", "pts"),
-        P(),
+        P("grid", "pts"),
     )
-    return jax.shard_map(
+    sharded = jax.shard_map(
         on_device,
         mesh=mesh,
         in_specs=placed,
         out_specs=(P("grid", "pts", None, None), P("grid", "pts", None, None)),
         check_vma=False,
     )
+
+    def run(probes, weights, brick_owner, brick_slot, counts, length_scale):
+        spread = jnp.broadcast_to(length_scale[None, :], brick_owner.shape[:1] + (mesh.shape["pts"],))
+        return sharded(probes, weights, brick_owner, brick_slot, counts, spread)
+
+    return run

time: 42.2 us -> 40.4 us (0.957)
  Pallas kernels: 40.7 us -> 38.9 us
    pallas_call x2, Pallas kernels: 40.7 us -> 38.9 us  [the longest x1 37.8 us: on_device(): pl.pallas_call(functools.partial(kernel, chunks), out_shape=(jax.ShapeDty...]
where the time goes in v4:
time: 40.4 us; the launch traced here: 40.3 us
  Pallas kernels  38.9 us (96%)
  between operations  1.36 us (3%)
    pallas_call x1, Pallas kernels, on_device(): pl.pallas_call(functools.partial(kernel, chunks), out_shape=(jax.ShapeDty...  37.8 us
    pallas_call x1, Pallas kernels, on_device(): pl.pallas_call(points_kernel, out_shape=(out, out), in_specs=[vmem, vmem,...  1.09 us

profile of v4, /device:TPU:1, one launch (start us, length us, event | category | flops | bytes accessed | tf_op | source)
XLA Modules:
  0.0 40.3 jit_solution(10388552851344268489)
XLA Ops:
  0.6 0.0 copy-start
  1.3 37.8 %covariance.1 = (f32[256,128]{1,0:T(8,128)S(1)}, f32[32,8,128]{2,1,0:T(8,128)S(1)}) custom-call(s32[1,32]{1,0:T(1,128)} %bitcast.10, s32[1,32]{1,0:T(1,128)} %slot_hbm.1, s32[1,32]{1,0:T(1,128)} %count_hbm.1, bf16[32,8,128]{2,1,0:T(8,128)(2,1)} %bitcast.9, bf16[32,64,128]{2,1,0:T(8,128)(2,1)} %bitcast.7, f32[1,1]{1,0:T(1,128)} %bitcast.6.scale_hbm), custom_call_target="tpu_custom_call" | custom-call | tf_op jit(solution)/shard_map/covariance/pallas_call | solution.py:277
  39.2 0.0 copy-done
  39.2 1.1 %points.1 = (f32[32,8,128]{2,1,0:T(8,128)}, f32[32,8,128]{2,1,0:T(8,128)}) custom-call(f32[32,8,128]{2,1,0:T(8,128)S(1)} %get-tuple-element.6.usable_ref, f32[256,128]{1,0:T(8,128)S(1)} %get-tuple-element.7.rows_ref, bf16[32,64,128]{2,1,0:T(8,128)(2,1)S(1)} %bitcast.8), custom_call_target="tpu_custom_call" | custom-call | tf_op jit(solution)/shard_map/points/pallas_call | solution.py:312
Async XLA Ops:
  0.6 38.5 %copy-start = (bf16[1,32,64,128]{3,2,1,0:T(8,128)(2,1)S(1)}, bf16[1,32,64,128]{3,2,1,0:T(8,128)(2,1)}, u32[]{:S(2)}) copy-start(bf16[1,32,64,128]{3,2,1,0:T(8,128)(2,1)} %param.7) | copy-start | bytes 1572868

commit v5 on v4

--- a/solution.py
+++ b/solution.py
@@ -178,10 +178,10 @@
     brick_y = wide[:, 64:65].astype(I32)
     brick_z = wide[:, 65:66].astype(I32)
     across = wide.T[0:64].astype(BF16)
-    lane256 = iota((PEERS * 16, 256), 1)
-    brick = brick_y * 32 + brick_z
+    brick = brick_y * 32 + brick_z - iota((PEERS * 16, 128), 1)
     for t in range(4):
-        there = (lane256 == brick - t * 256).astype(F32).astype(BF16)
+        pair = [(brick == t * 256).astype(F32), (brick == t * 256 + 128).astype(F32)]
+        there = jnp.concatenate(pair, axis=1).astype(BF16)
         cells = dot(across, there)
         placed[pl.ds(t * 128, 64), :] = cells[:, 0:128]
         placed[pl.ds(t * 128 + 64, 64), :] = cells[:, 128:256]
@@ -255,14 +255,21 @@
 
 def points_kernel(usable_ref, rows_ref, weight_ref, cov_ref, adj_ref):
     lane8 = iota((8, 128), 1)
-    for b in range(weight_ref.shape[0]):
-        block = rows_ref[pl.ds(b * 8, 8), :]
-        both = jnp.concatenate([jnp.where(lane8 < 64, block, 0.0), jnp.where(lane8 < 64, 0.0, block)], axis=0)
-        twice = jnp.concatenate([weight_ref[b], weight_ref[b]], axis=0)
-        result = dot(both.astype(BF16), twice)
-        usable = usable_ref[b] > 0.0
-        cov_ref[b] = jnp.where(usable, result[0:8], 0.0)
-        adj_ref[b] = jnp.where(usable, result[8:16], 0.0)
+    left = lane8 < 64
+    for b in range(0, weight_ref.shape[0], 2):
+        first, second = rows_ref[pl.ds(b * 8, 8), :], rows_ref[pl.ds(b * 8 + 8, 8), :]
+        four = jnp.concatenate(
+            [
+                jnp.where(left, first, 0.0), jnp.where(left, pltpu.roll(first, 64, 1), 0.0),
+                jnp.where(left, 0.0, pltpu.roll(second, 64, 1)), jnp.where(left, 0.0, second),
+            ],
+            axis=0,
+        )
+        result = dot(four.astype(BF16), weight_ref[pl.ds(b, 2)].reshape(128, 128))
+        for u in range(2):
+            usable = usable_ref[b + u] > 0.0
+            cov_ref[b + u] = jnp.where(usable, result[u * 16 : u * 16 + 8], 0.0)
+            adj_ref[b + u] = jnp.where(usable, result[u * 16 + 8 : u * 16 + 16], 0.0)
 
 
 CHUNKS = 4

time: 40.4 us -> 40.2 us (level)
  no operation moved by 1% of the time
where the time goes in v5:
time: 40.2 us; the launch traced here: 40 us
  Pallas kernels  38.7 us (96%)
  between operations  1.36 us (3%)
    pallas_call x1, Pallas kernels, on_device(): pl.pallas_call(functools.partial(kernel, chunks), out_shape=(jax.ShapeDty...  37.7 us
    pallas_call x1, Pallas kernels, on_device(): pl.pallas_call(points_kernel, out_shape=(out, out), in_specs=[vmem, vmem,...  1.01 us

profile of v5, /device:TPU:1, one launch (start us, length us, event | category | flops | bytes accessed | tf_op | source)
XLA Modules:
  0.0 40.0 jit_solution(6315629105204506219)
XLA Ops:
  0.6 0.0 copy-start
  1.3 37.7 %covariance.1 = (f32[256,128]{1,0:T(8,128)S(1)}, f32[32,8,128]{2,1,0:T(8,128)S(1)}) custom-call(s32[1,32]{1,0:T(1,128)} %bitcast.10, s32[1,32]{1,0:T(1,128)} %slot_hbm.1, s32[1,32]{1,0:T(1,128)} %count_hbm.1, bf16[32,8,128]{2,1,0:T(8,128)(2,1)} %bitcast.9, bf16[32,64,128]{2,1,0:T(8,128)(2,1)} %bitcast.7, f32[1,1]{1,0:T(1,128)} %bitcast.6.scale_hbm), custom_call_target="tpu_custom_call" | custom-call | tf_op jit(solution)/shard_map/covariance/pallas_call | solution.py:284
  39.0 0.0 copy-done
  39.0 1.0 %points.1 = (f32[32,8,128]{2,1,0:T(8,128)}, f32[32,8,128]{2,1,0:T(8,128)}) custom-call(f32[32,8,128]{2,1,0:T(8,128)S(1)} %get-tuple-element.6.usable_ref, f32[256,128]{1,0:T(8,128)S(1)} %get-tuple-element.7.rows_ref, bf16[32,64,128]{2,1,0:T(8,128)(2,1)S(1)} %bitcast.8), custom_call_target="tpu_custom_call" | custom-call | tf_op jit(solution)/shard_map/points/pallas_call | solution.py:319
Async XLA Ops:
  0.6 38.4 %copy-start = (bf16[1,32,64,128]{3,2,1,0:T(8,128)(2,1)S(1)}, bf16[1,32,64,128]{3,2,1,0:T(8,128)(2,1)}, u32[]{:S(2)}) copy-start(bf16[1,32,64,128]{3,2,1,0:T(8,128)(2,1)} %param.7) | copy-start | bytes 1572868

commit v6 on v5

--- a/solution.py
+++ b/solution.py
@@ -14,6 +14,7 @@
 BF16 = jnp.bfloat16
 I32 = jnp.int32
 PEERS = 32
+NEAR = ((2, 0), (6, 0), (2, 1), (6, 1), (0, 1))
 
 
 def iota(shape, dim):
@@ -47,7 +48,7 @@
     chunks, owner_hbm, slot_hbm, count_hbm, probe_hbm, weight_hbm, scale_hbm, rows_ref, usable_ref,
     owner_ref, slot_ref, count_ref, scale_ref, probe_ref, weight_ref, sums, sel, slots, placed, lines, field, gather, total,
     send1, recv1, send2, recv2, send3, recv3, send4, recv4,
-    send_sem, recv_sem, load_sem,
+    send_sem, recv_sem, load_sem, slab_sem, all_sem,
 ):
     g = lax.axis_index("grid")
     i = lax.axis_index("pts")
@@ -78,10 +79,11 @@
         to_g = (z // 2) * 2 + lax.rem(core + shift[2], 2)
         return to_g * 4 + place, {"grid": to_g, "pts": probe * 4 + place}
 
+    near = [{"grid": lax.rem(g + hop, 8) // 2 * 2 + lax.rem(core + swap, 2), "pts": i} for hop, swap in NEAR]
     barrier = pltpu.get_barrier_semaphore()
-    for peer, shifts in ((line_peer, line_shifts), (pts_peer, pts_shifts)):
-        for shift in shifts:
-            pl.semaphore_signal(barrier, inc=1, device_id=peer(shift)[1], device_id_type=pl.DeviceIdType.MESH)
+    greeted = [pts_peer(shift)[1] for shift in pts_shifts[:16]] + near + [pts_peer(shift)[1] for shift in pts_shifts[16:]]
+    for device in greeted:
+        pl.semaphore_signal(barrier, inc=1, device_id=device, device_id_type=pl.DeviceIdType.MESH)
 
     loads = [
         pltpu.make_async_copy(source, target, load_sem.at[n])
@@ -154,8 +156,10 @@
     message = dot(spread, sums[...].astype(BF16))
     send1[...] = message.astype(BF16).reshape(PEERS, 16, 128)
 
-    pl.semaphore_wait(barrier, 2 * (PEERS - 1))
+    pl.semaphore_wait(barrier, PEERS - 1 + len(NEAR))
     start(0, i, pts_peer, pts_shifts, send1, recv1)
+    for device in near:
+        pl.semaphore_signal(slab_sem, inc=1, device_id=device, device_id_type=pl.DeviceIdType.MESH)
 
     row_z, lane_z = iota((128, 256), 0), iota((128, 256), 1)
     value, slope = matern(jnp.abs(swapped(row_z) - swapped(lane_z % 128)).astype(F32), ell)
@@ -172,6 +176,8 @@
     table_x = jnp.where(out_slope == in_mixed, value, jnp.where(out_slope == 1, slope, 0.0))
     along_x = jnp.concatenate(split(table_x), axis=1)
 
+    pl.semaphore_wait(slab_sem, len(NEAR))
+    pl.semaphore_signal(all_sem, inc=1, device_id=near[0], device_id_type=pl.DeviceIdType.MESH)
     whole(0, send1, recv1).wait_recv()
 
     wide = recv1[...].reshape(PEERS * 16, 128).astype(F32)
@@ -202,6 +208,7 @@
         by_y = dot(along_y, jnp.concatenate([part, part], axis=0))
         field[pl.ds(cx, 128, stride=8), :] = by_y[0:128, 0:128]
         field[pl.ds(4 + cx, 128, stride=8), :] = by_y[0:128, 128:256] + by_y[128:256, 0:128]
+    pl.semaphore_wait(all_sem, 1)
     for c in range(chunks):
         for k in range(per):
             cy = c * per + k
@@ -305,6 +312,8 @@
             pltpu.SemaphoreType.DMA((2 + 2 * chunks,)),
             pltpu.SemaphoreType.DMA((2 + 2 * chunks,)),
             pltpu.SemaphoreType.DMA((6,)),
+            pltpu.SemaphoreType.REGULAR,
+            pltpu.SemaphoreType.REGULAR,
         ],
         compiler_params=pltpu.CompilerParams(collective_id=0, has_side_effects=True, vmem_limit_bytes=24 << 20),
         name="covariance",

time: 40.2 us -> 40.2 us (level)
  no operation moved by 1% of the time
where the time goes in v6:
time: 40.2 us; the launch traced here: 40.1 us
  Pallas kernels  38.7 us (96%)
  between operations  1.36 us (3%)
    pallas_call x1, Pallas kernels, on_device(): pl.pallas_call(functools.partial(kernel, chunks), out_shape=(jax.ShapeDty...  37.7 us
    pallas_call x1, Pallas kernels, on_device(): pl.pallas_call(points_kernel, out_shape=(out, out), in_specs=[vmem, vmem,...  1.01 us

profile of v6, /device:TPU:1, one launch (start us, length us, event | category | flops | bytes accessed | tf_op | source)
XLA Modules:
  0.0 40.1 jit_solution(10464628491938085875)
XLA Ops:
  0.6 0.0 copy-start
  1.3 37.7 %covariance.1 = (f32[256,128]{1,0:T(8,128)S(1)}, f32[32,8,128]{2,1,0:T(8,128)S(1)}) custom-call(s32[1,32]{1,0:T(1,128)} %bitcast.10, s32[1,32]{1,0:T(1,128)} %slot_hbm.1, s32[1,32]{1,0:T(1,128)} %count_hbm.1, bf16[32,8,128]{2,1,0:T(8,128)(2,1)} %bitcast.9, bf16[32,64,128]{2,1,0:T(8,128)(2,1)} %bitcast.7, f32[1,1]{1,0:T(1,128)} %bitcast.6.scale_hbm), custom_call_target="tpu_custom_call" | custom-call | tf_op jit(solution)/shard_map/covariance/pallas_call | solution.py:291
  39.1 0.0 copy-done
  39.1 1.0 %points.1 = (f32[32,8,128]{2,1,0:T(8,128)}, f32[32,8,128]{2,1,0:T(8,128)}) custom-call(f32[32,8,128]{2,1,0:T(8,128)S(1)} %get-tuple-element.6.usable_ref, f32[256,128]{1,0:T(8,128)S(1)} %get-tuple-element.7.rows_ref, bf16[32,64,128]{2,1,0:T(8,128)(2,1)S(1)} %bitcast.8), custom_call_target="tpu_custom_call" | custom-call | tf_op jit(solution)/shard_map/points/pallas_call | solution.py:328
Async XLA Ops:
  0.6 38.4 %copy-start = (bf16[1,32,64,128]{3,2,1,0:T(8,128)(2,1)S(1)}, bf16[1,32,64,128]{3,2,1,0:T(8,128)(2,1)}, u32[]{:S(2)}) copy-start(bf16[1,32,64,128]{3,2,1,0:T(8,128)(2,1)} %param.7) | copy-start | bytes 1572868
